TPU v7x, 256 devices: a whole 4x4x8 slice. The times are simulated.
256 devices in a mesh: ep: 64 (over y, z, core), fs: 4 (over x).
Axes of the slice: x: 4, y: 4, z: 8, core: 2. Of those that a mesh axis runs over, the one named last changes fastest.
Arguments:
- tokens: bfloat16 [8192, 4096], P('ep', 'fs'), may hold values from -6 to 6
- grad_out: bfloat16 [8192, 4096], P('ep', 'fs'), may hold values from -6 to 6
- gate_weight: bfloat16 [4, 14336, 4096], P('fs', 'ep'), may hold values from -0.09375 to 0.09375
- up_weight: bfloat16 [4, 14336, 4096], P('fs', 'ep'), may hold values from -0.09375 to 0.09375
- down_weight: bfloat16 [4, 14336, 4096], P('fs', 'ep'), may hold values from -0.046875 to 0.046875
- gate_values: float32 [4, 256], P('fs'), may hold values from 0.25 to 1
- chosen: int32 [4, 256], replicated, may hold values from 0 to 8191, as said below
- counts: int32 [4], replicated, may hold values from 128 to 256, as said below
Outputs:
- gate_grad: bfloat16 [4, 14336, 4096], P('fs', 'ep')
- up_grad: bfloat16 [4, 14336, 4096], P('fs', 'ep')
- down_grad: bfloat16 [4, 14336, 4096], P('fs', 'ep')
- token_grad: bfloat16 [8192, 4096], P('ep', 'fs')
- score_grad: float32 [4, 256], P('fs')
Inputs may be any that keep to these rules, and one draw needn't show every extreme that they name: `chosen`: the 256 entries of one row are distinct tokens; only the first counts[e] entries of row e are live, the others are padding to be ignored. Among the live entries of one expert at most 6 lie in one aligned block of 128 tokens (the tokens of one index of ep), and in every draw every expert has exactly 6 live entries in some block. `counts`: some expert has all 256 entries live in every draw.
All inputs are finite; a program needn't handle non-finite values.
Results may differ from a plain program's by a relative error of at most 0.0057.
Values may be sent and summed in bfloat16 or wider, within the bound.
No kernel may reach another device: no remote copies, remote signals or barrier semaphores. Data moves between devices by JAX's collectives and lax.ppermute only.
A program may use at most 128 MiB of HBM per device.

v0:
```python
import jax
import jax.numpy as jnp
from jax import lax
from jax.sharding import PartitionSpec as P

SLOTS = 6


def row_products(x_rows, dy_rows, gate_rows, gate_w, up_w, down_w):
    pre_gate = jnp.einsum("rd,hd->rh", x_rows, gate_w, preferred_element_type=jnp.float32)
    pre_up = jnp.einsum("rd,hd->rh", x_rows, up_w, preferred_element_type=jnp.float32)
    sigmoid_val = jax.nn.sigmoid(pre_gate)
    swished = pre_gate * sigmoid_val
    active = (swished * pre_up).astype(jnp.bfloat16)
    probes = jnp.einsum("rd,hd->rh", dy_rows, down_w, preferred_element_type=jnp.float32)
    score_term = jnp.sum(active.astype(jnp.float32) * probes, axis=1)
    weighted = (gate_rows[:, None] * dy_rows.astype(jnp.float32)).astype(jnp.bfloat16)
    d_active = gate_rows[:, None] * probes
    d_gate = (d_active * pre_up * sigmoid_val * (1.0 + pre_gate * (1.0 - sigmoid_val))).astype(
        jnp.bfloat16
    )
    d_up = (d_active * swished).astype(jnp.bfloat16)
    return (active, weighted, d_gate, d_up, score_term)


def weight_grads(stored):
    x_store, weighted_store, active_store, gate_store, up_store = (
        stored[0],
        stored[1],
        stored[2],
        stored[3],
        stored[4],
    )
    grad_g = jnp.einsum("rh,rd->hd", gate_store, x_store, preferred_element_type=jnp.float32)
    grad_u = jnp.einsum("rh,rd->hd", up_store, x_store, preferred_element_type=jnp.float32)
    grad_d = jnp.einsum(
        "rh,rd->hd", active_store, weighted_store, preferred_element_type=jnp.float32
    )
    return (grad_g, grad_u, grad_d)


def input_rows(stored_gate, stored_up, gate_w, up_w):

    def term_rows(row_start, row_count):
        return jnp.dot(stored_gate, gate_w, preferred_element_type=jnp.float32) + jnp.dot(
            stored_up, up_w, preferred_element_type=jnp.float32
        )

    return term_rows


def on_device(tokens, grad_out, gate_weight, up_weight, down_weight, gate_values, chosen, counts):
    ep_count = lax.axis_size("ep")
    ep_index = lax.axis_index("ep")
    fs_index = lax.axis_index("fs")
    tok_rows = tokens.shape[0]
    quarter = tokens.shape[1]
    experts_here = chosen.shape[0]
    total_slots = ep_count * SLOTS
    live = lax.broadcasted_iota(jnp.int32, chosen.shape, 1) < counts[:, None]
    shard_of = chosen // tok_rows
    block_iota = lax.broadcasted_iota(jnp.int32, (1, 1, ep_count), 2)
    one_hot = ((shard_of[:, :, None] == block_iota) & live[:, :, None]).astype(jnp.int32)
    ranks = jnp.sum((jnp.cumsum(one_hot, axis=1) - one_hot) * one_hot, axis=2)
    slot_pos = jnp.where(live, shard_of * SLOTS + ranks, total_slots)
    expert_ids = lax.broadcasted_iota(jnp.int32, chosen.shape, 0)
    slot_token = (
        jnp.full((experts_here, total_slots), -1, jnp.int32)
        .at[expert_ids, slot_pos]
        .set(chosen, mode="drop")
    )
    own_slots = lax.dynamic_slice_in_dim(slot_token, ep_index * SLOTS, SLOTS, 1)
    has_row = own_slots >= 0
    local_rows = jnp.where(has_row, own_slots - ep_index * tok_rows, 0)
    zero_val = jnp.zeros((), tokens.dtype)
    picked_x = jnp.where(has_row[:, :, None], tokens[local_rows], zero_val)
    picked_dy = jnp.where(has_row[:, :, None], grad_out[local_rows], zero_val)
    own_pos = lax.dynamic_index_in_dim(slot_pos, fs_index, 0, keepdims=False)
    own_live = lax.dynamic_index_in_dim(live, fs_index, 0, keepdims=False)
    slot_gate = jnp.zeros((total_slots,), jnp.float32).at[own_pos].set(gate_values[0], mode="drop")
    gate_w = gate_weight[0]
    up_w = up_weight[0]
    down_w = down_weight[0]
    gathered_x, gathered_dy = (
        lax.all_gather(picked_x, "ep", axis=1, tiled=True),
        lax.all_gather(picked_dy, "ep", axis=1, tiled=True),
    )
    whole_x, whole_dy = (
        lax.all_to_all(gathered_x, "fs", split_axis=0, concat_axis=2, tiled=True),
        lax.all_to_all(gathered_dy, "fs", split_axis=0, concat_axis=2, tiled=True),
    )
    x_rows = whole_x[0]
    dy_rows = whole_dy[0]
    active, weighted, d_gate, d_up, score_term = row_products(
        x_rows, dy_rows, slot_gate, gate_w, up_w, down_w
    )
    stored = (x_rows, weighted, active, d_gate, d_up, score_term)
    term_rows = input_rows(stored[3], stored[4], gate_w, up_w)
    partial_rows = term_rows(0, total_slots)
    spread = lax.all_to_all(partial_rows[None], "fs", split_axis=2, concat_axis=0, tiled=True)
    grad_g, grad_u, grad_d = weight_grads(stored)
    returned = lax.psum_scatter(spread, "ep", scatter_dimension=1, tiled=True)
    score_sum = lax.psum(stored[5], "ep")
    safe_pos = jnp.minimum(own_pos, total_slots - 1)
    score_grad = jnp.where(own_live, score_sum[safe_pos], 0.0)[None]
    targets = jnp.where(has_row, local_rows, tok_rows).reshape(-1)
    token_sum = (
        jnp.zeros((tok_rows, quarter), jnp.float32)
        .at[targets]
        .add(returned.reshape(-1, quarter), mode="drop")
    )
    token_grad = token_sum.astype(jnp.bfloat16)
    return (
        grad_g.astype(jnp.bfloat16)[None],
        grad_u.astype(jnp.bfloat16)[None],
        grad_d.astype(jnp.bfloat16)[None],
        token_grad,
        score_grad,
    )


def solution(mesh):
    return jax.shard_map(
        on_device,
        mesh=mesh,
        in_specs=(
            P("ep", "fs"),
            P("ep", "fs"),
            P("fs", "ep", None),
            P("fs", "ep", None),
            P("fs", "ep", None),
            P("fs", None),
            P(),
            P(),
        ),
        out_specs=(
            P("fs", "ep", None),
            P("fs", "ep", None),
            P("fs", "ep", None),
            P("ep", "fs"),
            P("fs", None),
        ),
        check_vma=False,
    )
```

profile of v0, /device:TPU:2, one launch (start us, length us, event | category | flops | bytes accessed | tf_op | source)
XLA Modules:
  0.0 556.3 jit_solution(6767352351725591109)
XLA Ops:
  7.2 0.8 iota_compare_fusion.2
  10.3 2.4 reduce-window.6
  13.1 0.8 fusion.23
  13.9 0.7 and_reduce_fusion
  15.4 4.3 scatter_custom_fusion.2
  20.0 1.6 gather_fusion.1
  21.6 1.6 gather_fusion
  24.8 80.4 %all-gather.5.cloned.1.call-done = bf16[4,384,1024]{2,0,1:T(4,128)(2,1)} async-done(((bf16[4,6,1024]{2,0,1:T(4,128)(2,1)}), bf16[4,384,1024]{2,0,1:T(4,128)(2,1)}) %all-gather.5.cloned.1.call-update) | async-done | bytes 3145744 | tf_op jit(solution)/shard_map/all_gather | solution.py:85
  105.2 6.3 %copy.26 = bf16[4,384,1024]{1,2,0:T(8,128)(2,1)} copy(bf16[4,384,1024]{2,0,1:T(4,128)(2,1)} %all-gather.5.cloned.1.call-done) | data formatting | bytes 6291456 | tf_op jit(solution)/shard_map/all_gather | solution.py:85
  111.5 5.2 all-to-all-start.1
  116.7 67.2 %all-gather.3.cloned.1.call-done = bf16[4,384,1024]{2,0,1:T(4,128)(2,1)} async-done(((bf16[4,6,1024]{2,0,1:T(4,128)(2,1)}), bf16[4,384,1024]{2,0,1:T(4,128)(2,1)}) %all-gather.3.cloned.1.call-update) | async-done | bytes 3145744 | tf_op jit(solution)/shard_map/all_gather | solution.py:86
  184.0 6.3 %copy.24 = bf16[4,384,1024]{1,2,0:T(8,128)(2,1)} copy(bf16[4,384,1024]{2,0,1:T(4,128)(2,1)} %all-gather.3.cloned.1.call-done) | data formatting | bytes 6291456 | tf_op jit(solution)/shard_map/all_gather | solution.py:86
  190.2 5.2 all-to-all-start
  195.4 1.6 scatter_custom_fusion
  197.0 3.6 fusion.9
  200.6 3.0 fusion.6
  203.6 28.7 %all-to-all-done = bf16[4,384,1024]{1,2,0:T(8,128)(2,1)} async-done(((bf16[4,384,1024]{1,2,0:T(8,128)(2,1)}), bf16[4,384,1024]{1,2,0:T(8,128)(2,1)}, u32[]{:S(2)}, u32[]{:S(2)}) %all-to-all-start) | async-done | bytes 3145760 | tf_op jit(solution)/shard_map/all_to_all | solution.py:90
  232.3 3.7 multiply_reduce_fusion
  236.0 1.0 fusion.4
  237.5 3.7 add_bitcast_fusion
  241.2 14.8 %copy.27 = f32[1,384,4096]{1,0,2:T(1,128)} copy(f32[1,384,4096]{2,1,0:T(8,128)} %add_bitcast_fusion) | data formatting | bytes 12582912 | tf_op jit(solution)/shard_map/broadcast_in_dim | solution.py:100
  255.9 77.8 %all_to_all.48 = f32[1,384,4096]{1,0,2:T(1,128)} all-to-all(f32[1,384,4096]{1,0,2:T(1,128)} %copy.27), channel_id=1, replica_groups=mesh['ep'=64,'fs'=4] {'fs'}, dimensions={2} | all-to-all | bytes 12582912 | tf_op jit(solution)/shard_map/all_to_all | solution.py:100
  333.7 15.9 %copy.28 = f32[1,384,4,1024]{3,2,1,0:T(4,128)} copy(f32[1,384,4,1024]{1,0,3,2:T(1,128)} %bitcast.91) | data formatting | bytes 12582912 | tf_op jit(solution)/shard_map/all_to_all | solution.py:100
  351.6 125.2 %psum.7 = f32[384]{0:T(512)S(1)} all-reduce(f32[384]{0:T(512)S(1)} %get-tuple-element.5), channel_id=1, replica_groups=mesh['ep'=64,'fs'=4] {'ep'}, use_global_device_ids=true, to_apply=%region_8.9 | all-reduce | flops 384 | bytes 3072 | tf_op jit(solution)/shard_map/psum | solution.py:103
  476.7 1.9 gather_fusion.2
  479.3 4.4 fusion
  483.7 4.4 fusion.1
  488.0 4.6 fusion.2
  492.6 54.5 %all-reduce.3.cloned.1.call-done = f32[4,384,1024]{2,0,1:T(4,128)} async-done(((f32[4,384,1024]{2,0,1:T(4,128)}), f32[4,384,1024]{2,0,1:T(4,128)}) %all-reduce.3.cloned.1.call-update) | async-done | bytes 6291472
  547.1 0.9 constant_dynamic-slice_fusion.1
  548.1 0.9 scatter_custom_fusion.1
  549.0 0.7 convert_element_type.47
  (49 shorter events, 7.6 us)
Async XLA Ops:
  7.2 193.4 %copy-start = (bf16[1,224,4096]{2,1,0:T(8,128)(2,1)S(1)}, bf16[1,224,4096]{2,1,0:T(8,128)(2,1)}, u32[]{:S(2)}) copy-start(bf16[1,224,4096]{2,1,0:T(8,128)(2,1)} %param.10) | copy-start | bytes 5505028
  7.2 98.0 %all-gather.5.cloned.1.call-start = ((), (), s32[]{:S(2)}) async-start(), calls=%async_computation.4 | async-start | bytes 3194880 | tf_op jit(solution)/shard_map/all_gather | solution.py:85
  24.1 159.9 %all-gather.3.cloned.1.call-start = ((), (), s32[]{:S(2)}) async-start(), calls=%async_computation.3 | async-start | bytes 3194880 | tf_op jit(solution)/shard_map/all_gather | solution.py:86
  111.5 78.7 %all-to-all-start.1 = ((bf16[4,384,1024]{1,2,0:T(8,128)(2,1)}), bf16[4,384,1024]{1,2,0:T(8,128)(2,1)}, u32[]{:S(2)}, u32[]{:S(2)}) async-start(bf16[4,384,1024]{1,2,0:T(8,128)(2,1)} %copy.26), calls=%async_computation.1 | async-start | bytes 6291456 | tf_op jit(solution)/shard_map/all_to_all | solution.py:89
  190.2 42.1 %all-to-all-start = ((bf16[4,384,1024]{1,2,0:T(8,128)(2,1)}), bf16[4,384,1024]{1,2,0:T(8,128)(2,1)}, u32[]{:S(2)}, u32[]{:S(2)}) async-start(bf16[4,384,1024]{1,2,0:T(8,128)(2,1)} %copy.24), calls=%async_computation | async-start | bytes 6291456 | tf_op jit(solution)/shard_map/all_to_all | solution.py:90
  195.4 351.7 %all-reduce.3.cloned.1.call-start = ((), (), s32[]{:S(2)}) async-start(), calls=%async_computation.5 | async-start | bytes 12582912
  236.0 1.5 copy-start.2
  349.6 0.7 copy-start.3
  488.0 61.7 %copy-start.1 = (bf16[1,224,4096]{2,1,0:T(8,128)(2,1)S(1)}, bf16[1,224,4096]{2,1,0:T(8,128)(2,1)}, u32[]{:S(2)}) copy-start(bf16[1,224,4096]{2,1,0:T(8,128)(2,1)} %param.10) | copy-start | bytes 5505028
Sparse Core Ops, SparseCore 0:
  24.2 80.9 all-gather.4
  108.5 75.3 all-gather.2
  349.8 197.2 all-reduce.2
where the time goes:
time: 558 us; the launch traced here: 556 us
  waiting for transfers between devices  231 us (41%)
  blocking collectives  203 us (36%)
  local copies, waits for them, and re-layouts  59.5 us (11%)
  matrix products  28.3 us (5%)
  between operations  14.6 us (3%)
  starting transfers between devices  10.5 us (2%)
  other arithmetic  9.64 us (2%)
    psum x1, blocking collectives, on_device(): score_sum = lax.psum(stored[5], 'ep')  125 us
    all_gather x1, waiting for transfers between devices, on_device(): lax.all_gather(picked_x, 'ep', axis=1, tiled=True)  80.4 us
    all_to_all x1, blocking collectives, on_device(): lax.all_to_all(partial_rows[None], 'fs', split_axis=2, concat_axis=0, til...  77.8 us
    all_gather x1, waiting for transfers between devices, on_device(): lax.all_gather(picked_dy, 'ep', axis=1, tiled=True)  67.2 us
    unnamed x4, waiting for transfers between devices  54.6 us
    all_to_all x1, waiting for transfers between devices, on_device(): lax.all_to_all(gathered_dy, 'fs', split_axis=0, concat_axis=2, tiled=True)  28.7 us
    all_to_all x1, local copies, waits for them, and re-layouts, on_device(): lax.all_to_all(partial_rows[None], 'fs', split_axis=2, concat_axis=0, til...  15.9 us
    broadcast_in_dim x1, local copies, waits for them, and re-layouts, on_device(): partial_rows[None]  14.8 us
  transfers between devices with their start and end apart: 5, of which 4 were waited for; matrix products, arithmetic and copies ran while one was open for 7% of the time, Pallas kernels for 0%

commit v1 on v0

--- a/solution.py
+++ b/solution.py
@@ -83,7 +83,9 @@
     down_w = down_weight[0]
     gathered_x, gathered_dy = (
         lax.all_gather(picked_x, "ep", axis=1, tiled=True),
-        lax.all_gather(picked_dy, "ep", axis=1, tiled=True),
+        jnp.concatenate(
+            lax.all_to_all(jnp.stack([picked_dy] * lax.axis_size("ep")), "ep", 0, 0), axis=1
+        ),
     )
     whole_x, whole_dy = (
         lax.all_to_all(gathered_x, "fs", split_axis=0, concat_axis=2, tiled=True),

time: 558 us -> 537 us (0.962)
  waiting for transfers between devices: 231 us -> 193 us
  starting transfers between devices: 10.5 us -> 23.6 us
  local copies, waits for them, and re-layouts: 59.5 us -> 65.2 us
    all_gather x1 -> x0, waiting for transfers between devices: 67.2 us -> none  [on_device(): lax.all_gather(picked_dy, 'ep', axis=1, tiled=True)]
    all_to_all x1, waiting for transfers between devices: 0.01 us -> 32.7 us  [on_device(): lax.all_to_all(gathered_x, 'fs', split_axis=0, concat_axis=2, tiled=True)]
    all_to_all x0 -> x1, starting transfers between devices: none -> 12.3 us  [on_device(): lax.all_to_all(jnp.stack([picked_dy] * lax.axis_size('ep')), 'ep', 0, 0)]
    all_gather x1 -> x0, local copies, waits for them, and re-layouts: 6.28 us -> none  [on_device(): lax.all_gather(picked_dy, 'ep', axis=1, tiled=True)]
    unnamed x4 -> x3, waiting for transfers between devices: 54.6 us -> 56.7 us
  transfers between devices with their start and end apart: 5 -> 5, of which waited for: 4 -> 5; matrix products, arithmetic and copies ran while one was open for 7% -> 7% of each run, Pallas kernels for 0% -> 0%
where the time goes in v1:
time: 537 us; the launch traced here: 535 us
  blocking collectives  202 us (38%)
  waiting for transfers between devices  193 us (36%)
  local copies, waits for them, and re-layouts  65.2 us (12%)
  matrix products  26.4 us (5%)
  starting transfers between devices  23.6 us (4%)
  between operations  14.9 us (3%)
  other arithmetic  9.64 us (2%)
    psum x1, blocking collectives, on_device(): score_sum = lax.psum(stored[5], 'ep')  125 us
    all_to_all x1, blocking collectives, on_device(): lax.all_to_all(partial_rows[None], 'fs', split_axis=2, concat_axis=0, til...  77.4 us
    all_gather x1, waiting for transfers between devices, on_device(): lax.all_gather(picked_x, 'ep', axis=1, tiled=True)  74.8 us
    unnamed x3, waiting for transfers between devices  56.7 us
    all_to_all x1, waiting for transfers between devices, on_device(): lax.all_to_all(gathered_x, 'fs', split_axis=0, concat_axis=2, tiled=True)  32.7 us
    all_to_all x1, waiting for transfers between devices, on_device(): lax.all_to_all(gathered_dy, 'fs', split_axis=0, concat_axis=2, tiled=True)  28.1 us
    all_to_all x1, local copies, waits for them, and re-layouts, on_device(): lax.all_to_all(partial_rows[None], 'fs', split_axis=2, concat_axis=0, til...  15.9 us
    broadcast_in_dim x1, local copies, waits for them, and re-layouts, on_device(): partial_rows[None]  14.8 us
  transfers between devices with their start and end apart: 5, of which 5 were waited for; matrix products, arithmetic and copies ran while one was open for 7% of the time, Pallas kernels for 0%

profile of v1, /device:TPU:2, one launch (start us, length us, event | category | flops | bytes accessed | tf_op | source)
XLA Modules:
  0.0 535.0 jit_solution(6158722877677808180)
XLA Ops:
  7.2 0.8 iota_compare_fusion.2
  10.3 2.4 reduce-window.6
  15.4 4.3 scatter_custom_fusion.2
  20.0 1.6 gather_fusion.1
  21.6 1.6 gather_fusion
  24.1 3.1 stack.2
  27.3 12.3 %all-to-all-start = ((bf16[64,4,6,1024]{3,1,2,0:T(4,128)(2,1)}), bf16[64,4,6,1024]{3,1,2,0:T(4,128)(2,1)}, u32[]{:S(2)}, u32[]{:S(2)}) async-start(bf16[64,4,6,1024]{3,1,2,0:T(4,128)(2,1)} %stack.2), calls=%async_computation | async-start | bytes 6291456 | tf_op jit(solution)/shard_map/all_to_all | solution.py:87
  39.6 74.8 %all-gather.2.cloned.1.call-done = bf16[4,384,1024]{2,0,1:T(4,128)(2,1)} async-done(((bf16[4,6,1024]{2,0,1:T(4,128)(2,1)}), bf16[4,384,1024]{2,0,1:T(4,128)(2,1)}) %all-gather.2.cloned.1.call-update) | async-done | bytes 3145744 | tf_op jit(solution)/shard_map/all_gather | solution.py:85
  114.4 6.3 %copy.28 = bf16[4,384,1024]{1,2,0:T(8,128)(2,1)} copy(bf16[4,384,1024]{2,0,1:T(4,128)(2,1)} %all-gather.2.cloned.1.call-done) | data formatting | bytes 6291456 | tf_op jit(solution)/shard_map/all_gather | solution.py:85
  121.6 5.2 all-to-all-start.2
  126.8 4.6 copy.25
  131.3 32.7 %all-to-all-done.2 = bf16[4,384,1024]{1,2,0:T(8,128)(2,1)} async-done(((bf16[4,384,1024]{1,2,0:T(8,128)(2,1)}), bf16[4,384,1024]{1,2,0:T(8,128)(2,1)}, u32[]{:S(2)}, u32[]{:S(2)}) %all-to-all-start.2) | async-done | bytes 3145760 | tf_op jit(solution)/shard_map/all_to_all | solution.py:91
  164.1 6.1 %all-to-all-start.1 = ((bf16[4,384,1024]{2,1,0:T(8,128)(2,1)}), bf16[4,384,1024]{2,1,0:T(8,128)(2,1)}, u32[]{:S(2)}, u32[]{:S(2)}) async-start(bf16[4,384,1024]{2,1,0:T(8,128)(2,1)} %copy.25), calls=%async_computation.1 | async-start | bytes 6291456 | tf_op jit(solution)/shard_map/all_to_all | solution.py:92
  170.1 1.7 scatter_custom_fusion
  171.9 3.6 fusion.9
  175.5 3.0 fusion.6
  178.5 28.1 %all-to-all-done.1 = bf16[4,384,1024]{2,1,0:T(8,128)(2,1)} async-done(((bf16[4,384,1024]{2,1,0:T(8,128)(2,1)}), bf16[4,384,1024]{2,1,0:T(8,128)(2,1)}, u32[]{:S(2)}, u32[]{:S(2)}) %all-to-all-start.1) | async-done | bytes 3145760 | tf_op jit(solution)/shard_map/all_to_all | solution.py:92
  206.6 4.7 copy.26
  211.3 3.7 multiply_reduce_fusion
  215.0 1.0 fusion.4
  216.5 3.7 add_bitcast_fusion
  220.2 14.8 %copy.29 = f32[1,384,4096]{1,0,2:T(1,128)} copy(f32[1,384,4096]{2,1,0:T(8,128)} %add_bitcast_fusion) | data formatting | bytes 12582912 | tf_op jit(solution)/shard_map/broadcast_in_dim | solution.py:102
  234.9 77.4 %all_to_all.53 = f32[1,384,4096]{1,0,2:T(1,128)} all-to-all(f32[1,384,4096]{1,0,2:T(1,128)} %copy.29), channel_id=1, replica_groups=mesh['ep'=64,'fs'=4] {'fs'}, dimensions={2} | all-to-all | bytes 12582912 | tf_op jit(solution)/shard_map/all_to_all | solution.py:102
  312.3 15.9 %copy.30 = f32[1,384,4,1024]{3,2,1,0:T(4,128)} copy(f32[1,384,4,1024]{1,0,3,2:T(1,128)} %bitcast.94) | data formatting | bytes 12582912 | tf_op jit(solution)/shard_map/all_to_all | solution.py:102
  330.2 124.7 %psum.7 = f32[384]{0:T(512)S(1)} all-reduce(f32[384]{0:T(512)S(1)} %get-tuple-element.5), channel_id=1, replica_groups=mesh['ep'=64,'fs'=4] {'ep'}, use_global_device_ids=true, to_apply=%region_8.9 | all-reduce | flops 384 | bytes 3072 | tf_op jit(solution)/shard_map/psum | solution.py:105
  454.9 1.9 gather_fusion.2
  457.4 4.4 fusion
  461.8 4.5 fusion.1
  466.3 2.5 fusion.2
  468.9 56.7 %all-reduce.3.cloned.1.call-done = f32[4,384,1024]{2,0,1:T(4,128)} async-done(((f32[4,384,1024]{2,0,1:T(4,128)}), f32[4,384,1024]{2,0,1:T(4,128)}) %all-reduce.3.cloned.1.call-update) | async-done | bytes 6291472
  525.6 0.9 constant_dynamic-slice_fusion.1
  526.5 0.9 scatter_custom_fusion.1
  (52 shorter events, 10.0 us)
Async XLA Ops:
  7.2 168.3 %copy-start = (bf16[1,224,4096]{2,1,0:T(8,128)(2,1)S(1)}, bf16[1,224,4096]{2,1,0:T(8,128)(2,1)}, u32[]{:S(2)}) copy-start(bf16[1,224,4096]{2,1,0:T(8,128)(2,1)} %param.10) | copy-start | bytes 5505028
  7.2 107.3 %all-gather.2.cloned.1.call-start = ((), (), s32[]{:S(2)}) async-start(), calls=%async_computation.4 | async-start | bytes 3194880 | tf_op jit(solution)/shard_map/all_gather | solution.py:85
  27.3 94.3 %all-to-all-start = ((bf16[64,4,6,1024]{3,1,2,0:T(4,128)(2,1)}), bf16[64,4,6,1024]{3,1,2,0:T(4,128)(2,1)}, u32[]{:S(2)}, u32[]{:S(2)}) async-start(bf16[64,4,6,1024]{3,1,2,0:T(4,128)(2,1)} %stack.2), calls=%async_computation | async-start | bytes 6291456 | tf_op jit(solution)/shard_map/all_to_all | solution.py:87
  121.6 42.5 %all-to-all-start.2 = ((bf16[4,384,1024]{1,2,0:T(8,128)(2,1)}), bf16[4,384,1024]{1,2,0:T(8,128)(2,1)}, u32[]{:S(2)}, u32[]{:S(2)}) async-start(bf16[4,384,1024]{1,2,0:T(8,128)(2,1)} %copy.28), calls=%async_computation.2 | async-start | bytes 6291456 | tf_op jit(solution)/shard_map/all_to_all | solution.py:91
  164.1 42.5 %all-to-all-start.1 = ((bf16[4,384,1024]{2,1,0:T(8,128)(2,1)}), bf16[4,384,1024]{2,1,0:T(8,128)(2,1)}, u32[]{:S(2)}, u32[]{:S(2)}) async-start(bf16[4,384,1024]{2,1,0:T(8,128)(2,1)} %copy.25), calls=%async_computation.1 | async-start | bytes 6291456 | tf_op jit(solution)/shard_map/all_to_all | solution.py:92
  170.1 355.4 %all-reduce.3.cloned.1.call-start = ((), (), s32[]{:S(2)}) async-start(), calls=%async_computation.5 | async-start | bytes 12582912
  215.0 1.5 copy-start.3
  328.2 0.7 copy-start.4
  461.8 4.5 copy-start.2
  466.3 61.9 %copy-start.1 = (bf16[1,224,4096]{2,1,0:T(8,128)(2,1)S(1)}, bf16[1,224,4096]{2,1,0:T(8,128)(2,1)}, u32[]{:S(2)}) copy-start(bf16[1,224,4096]{2,1,0:T(8,128)(2,1)} %param.10) | copy-start | bytes 5505028
Sparse Core Ops, SparseCore 0:
  24.2 90.1 all-gather.1
  328.4 197.1 all-reduce.2
